TPU v7x, 32 devices: a whole 2x2x4 slice. The times are simulated.
32 devices in a mesh: dp: 4 (over y, x), mp: 8 (over z, core).
Axes of the slice: x: 2, y: 2, z: 4, core: 2. Of those that a mesh axis runs over, the one named last changes fastest.
Arguments:
- tokens: bfloat16 [1024, 8192], P('dp', 'mp'), may hold values from -6 to 6
- base_weight: bfloat16 [24576, 8192], P('mp'), may hold values from -0.0625 to 0.0625
- block_values: bfloat16 [256, 128, 128], P('mp'), may hold values from -0.0625 to 0.0625
- block_ids: int32 [2, 256], P(None, 'mp'), may hold values from -1 to 63, as said below
- lowrank_model: float32 [8192, 256], P('mp'), may hold values from -6 to 6
- lowrank_hidden: float32 [24576, 256], P('mp'), may hold values from -6 to 6
- output_cotangent: bfloat16 [1024, 24576], P('dp', 'mp'), may hold values from -6 to 6
Outputs:
- projection_output: bfloat16 [1024, 24576], P('dp', 'mp')
- input_cotangent: bfloat16 [1024, 8192], P('dp', 'mp')
- block_grads: float32 [256, 128, 128], P(('mp', 'dp'))
- updated_model: float32 [8192, 256], P('mp')
- updated_hidden: float32 [24576, 256], P('mp')
Inputs may be any that keep to these rules, and one draw needn't show every extreme that they name: `block_ids`: slots 32 * m to 32 * (m + 1) - 1 belong to index m of mp. A live slot has row 0 in 0 to 23 and row 1 in 0 to 63; the live slots of one index come first and name distinct blocks; the remaining slots hold -1 in both rows. Every index has 8 or more live slots, and some index has all 32.
All inputs are finite; a program needn't handle non-finite values.
Results may differ from a plain program's by a relative error of at most 0.0065.
Values may be sent and summed in bfloat16 or wider, within the bound.
A program may use at most 384 MiB of HBM per device.

v0:
```python
import math
import jax
import jax.numpy as jnp
from jax import lax
from jax.sharding import PartitionSpec as P


def partner_2(value, axis, distance):
    return lax.ppermute(value, axis, [(i, i ^ 1 << distance) for i in range(lax.axis_size(axis))])


def shards(
    tokens, base_weight, block_values, block_ids, lowrank_model, lowrank_hidden, output_cotangent
):
    tok_rows = tokens.shape[0]
    mp_size = lax.axis_size("mp")
    dp_size = lax.axis_size("dp")
    total_tokens = tok_rows * dp_size
    f_local = base_weight.shape[0]
    feature_width = base_weight.shape[1]
    hidden_total = f_local * mp_size
    nb_local = block_values.shape[0]
    block_size = block_values.shape[1]
    adapter_factor_rank = lowrank_model.shape[1]
    col_blocks = feature_width // block_size
    row_blocks = f_local // block_size
    adapter_scale = 0.5 / math.sqrt(adapter_factor_rank * feature_width)
    row_ids = block_ids[0]
    col_ids = block_ids[1]
    live_slots = row_ids >= 0
    flat_index = jnp.where(live_slots, row_ids * col_blocks + col_ids, -1)
    placer = (
        flat_index[:, None] == jnp.arange(row_blocks * col_blocks, dtype=jnp.int32)[None, :]
    ).astype(jnp.bfloat16)
    dense_blocks = lax.dot_general(
        placer,
        block_values.reshape(nb_local, block_size * block_size),
        (((0,), (0,)), ((), ())),
        preferred_element_type=jnp.float32,
    )
    dense_blocks = (
        dense_blocks.reshape(row_blocks, col_blocks, block_size, block_size)
        .transpose(0, 2, 1, 3)
        .reshape(f_local, feature_width)
    )
    effective = (base_weight.astype(jnp.float32) + dense_blocks).astype(jnp.bfloat16)
    gathered = lax.all_gather(tokens, "mp", axis=1, tiled=True)
    model_half = lowrank_model.astype(jnp.bfloat16)
    hidden_half = lowrank_hidden.astype(jnp.bfloat16)
    v_partial = jnp.dot(output_cotangent, hidden_half, preferred_element_type=jnp.float32)
    model_rows = lax.all_gather(model_half, "mp", axis=0, tiled=True)
    u_summed = jnp.dot(gathered, model_rows, preferred_element_type=jnp.float32)
    v_summed = lax.psum(v_partial, "mp")
    left_factor_shard = u_summed.astype(jnp.bfloat16)
    right_factor_shard = v_summed.astype(jnp.bfloat16)
    base_projection_output = lax.dot_general(
        gathered, effective, (((1,), (1,)), ((), ())), preferred_element_type=jnp.float32
    )
    lowrank_output = lax.dot_general(
        left_factor_shard, hidden_half, (((1,), (1,)), ((), ())), preferred_element_type=jnp.float32
    )
    projection_output = (base_projection_output + adapter_scale * lowrank_output).astype(
        jnp.bfloat16
    )
    backward_lowrank_term = lax.dot_general(
        right_factor_shard, model_half, (((1,), (1,)), ((), ())), preferred_element_type=jnp.float32
    )
    backward_base_term = lax.psum_scatter(
        lax.dot_general(
            effective,
            output_cotangent,
            (((0,), (1,)), ((), ())),
            preferred_element_type=jnp.float32,
        ),
        "mp",
        scatter_dimension=0,
        tiled=True,
    ).T
    input_cotangent = (backward_base_term + adapter_scale * backward_lowrank_term).astype(
        jnp.bfloat16
    )
    right_factor_gradient_part = adapter_scale * lax.dot_general(
        output_cotangent,
        left_factor_shard,
        (((0,), (0,)), ((), ())),
        preferred_element_type=jnp.float32,
    )
    left_factor_gradient_part = adapter_scale * lax.dot_general(
        tokens, right_factor_shard, (((0,), (0,)), ((), ())), preferred_element_type=jnp.float32
    )
    hidden_side_gradient, model_side_gradient = (
        lax.psum(right_factor_gradient_part.astype(jnp.bfloat16), "dp").astype(jnp.float32),
        lax.psum(left_factor_gradient_part.astype(jnp.bfloat16), "dp").astype(jnp.float32),
    )
    safe_rows = jnp.maximum(row_ids, 0)
    safe_cols = jnp.maximum(col_ids, 0)
    grad_sel = jnp.take(
        output_cotangent.reshape(tok_rows, row_blocks, block_size), safe_rows, axis=1
    )
    token_sel = jnp.take(gathered.reshape(tok_rows, col_blocks, block_size), safe_cols, axis=1)
    block_part = jnp.einsum("tbi,tbj->bij", grad_sel, token_sel, preferred_element_type=jnp.float32)
    block_part = (
        block_part * (live_slots.astype(jnp.float32) / math.sqrt(total_tokens))[:, None, None]
    )
    block_grads = lax.psum_scatter(block_part, "dp", scatter_dimension=0, tiled=True)
    model_step = (
        lowrank_model
        - math.sqrt(adapter_factor_rank * feature_width / (total_tokens * hidden_total))
        * model_side_gradient
    )
    moved_hidden = (
        lowrank_hidden - math.sqrt(adapter_factor_rank / total_tokens) * hidden_side_gradient
    )
    gram_local = lax.dot_general(
        moved_hidden, moved_hidden, (((0,), (0,)), ((), ())), precision=lax.Precision.HIGHEST
    )
    lower_factor = jnp.linalg.cholesky(gram_local)
    levels = mp_size.bit_length() - 1
    for bit_index in range(levels):
        partner = partner_2(lower_factor.astype(jnp.bfloat16), "mp", bit_index).astype(
            lower_factor.dtype
        )
        own_gram = jnp.dot(lower_factor, lower_factor.T, precision=lax.Precision.HIGHEST)
        partner_gram = jnp.dot(partner, partner.T, precision=lax.Precision.HIGHEST)
        lower_factor = jnp.linalg.cholesky(own_gram + partner_gram)
    solved = lax.linalg.triangular_solve(
        lower_factor, moved_hidden, left_side=False, lower=True, transpose_a=True
    )
    updated_hidden = math.sqrt(hidden_total) * solved
    updated_model = jnp.dot(model_step, lower_factor, precision=lax.Precision.HIGHEST) / math.sqrt(
        hidden_total
    )
    return (projection_output, input_cotangent, block_grads, updated_model, updated_hidden)


def solution(mesh):
    in_specs = (
        P("dp", "mp"),
        P("mp", None),
        P("mp", None, None),
        P(None, "mp"),
        P("mp", None),
        P("mp", None),
        P("dp", "mp"),
    )
    out_specs = (
        P("dp", "mp"),
        P("dp", "mp"),
        P(("mp", "dp"), None, None),
        P("mp", None),
        P("mp", None),
    )
    return jax.shard_map(shards, mesh=mesh, in_specs=in_specs, out_specs=out_specs, check_vma=False)
```

profile of v0, /device:TPU:0, one launch (start us, length us, event | category | flops | bytes accessed | tf_op | source)
XLA Modules:
  0.0 534.8 jit_solution(5461947114065312162)
XLA Ops:
  7.2 2.2 copy.48
  9.5 2.1 convert_element_type.59
  11.6 2.0 fusion.29
  14.3 39.6 %all-reduce.6 = bf16[256,256]{1,0:T(8,128)(2,1)S(1)} all-reduce(f32[256,256]{1,0:T(8,128)S(1)} %fusion.29), channel_id=1, replica_groups=mesh['dp'=4,'mp'=8] {'mp'}, use_global_device_ids=true, to_apply=%region_1.2 | all-reduce | flops 65536 | bytes 393216 | tf_op jit(solution)/shard_map/psum | solution.py:53
  53.9 2.2 fusion.22
  56.1 37.0 %fusion.23 = f32[24,64,128,128]{3,1,2,0:T(8,128)} fusion(s32[24,64]{1,0:T(8,128)S(1)} %multiply_add_fusion, s32[32]{0:T(128)S(1)} %get-tuple-element.61, bf16[4,8,128,128]{3,2,1,0:T(8,128)(2,1)} %bitcast.154), kind=kOutput, calls=%fused_computation.40 | convolution fusion | flops 1610661888 | bytes 101718144 | tf_op jit(solution)/shard_map/dot_general | solution.py:35
  93.1 19.2 %all-gather.5.cloned.1.call-done = bf16[8192,256]{1,0:T(8,128)(2,1)} async-done(((bf16[1024,256]{1,0:T(8,128)(2,1)}), bf16[8192,256]{1,0:T(8,128)(2,1)}) %all-gather.5.cloned.1.call-update) | async-done | bytes 4194320 | tf_op jit(solution)/shard_map/all_gather | solution.py:51
  112.3 4.9 convolution_convert_fusion
  117.2 1.9 fusion.4
  119.4 56.7 %fusion.106 = f32[8192,256]{1,0:T(8,128)} fusion(bf16[256,3072]{1,0:T(8,128)(2,1)} %param.14, f32[384,8,64,128]{3,2,1,0:T(8,128)} %bitcast.42, bf16[3072,8192]{1,0:T(8,128)(2,1)} %param.9), kind=kOutput, calls=%fused_computation.165 | convolution fusion | flops 12960399360 | bytes 160956416 | tf_op jit(solution)/shard_map/dot_general | solution.py:69
  176.1 2.6 copy.51
  178.8 2.6 copy.52
  181.4 3.6 gather_fusion
  185.0 91.2 %convolution_bitcast_fusion = f32[256,3072]{0,1:T(8,128)} fusion(bf16[256,8192]{0,1:T(8,128)(2,1)} %all-gather.3.cloned.1.call-done, f32[384,8,64,128]{3,2,1,0:T(8,128)} %bitcast.42, bf16[3072,8192]{1,0:T(8,128)(2,1)} %param.9), kind=kOutput, calls=%fused_computation.6 | convolution fusion | flops 12960399360 | bytes 158334976 | tf_op jit(solution)/shard_map/dot_general | solution.py:56
  276.2 3.7 fusion.2
  279.9 2.6 copy.67
  282.4 6.8 %copy.53 = bf16[256,64,128]{2,0,1:T(8,128)(2,1)} copy(bf16[256,64,128]{0,2,1:T(8,128)(2,1)} %bitcast.152) | data formatting | bytes 8388608 | tf_op jit(solution)/shard_map/reshape | solution.py:100
  289.3 4.5 gather_fusion.1
  293.8 3.9 fusion.14
  297.7 2.7 multiply_subtract_fusion
  300.4 5.1 fusion.110
  308.1 11.7 %cholesky.214 = f32[128,128]{1,0:T(8,128)S(1)} custom-call(f32[128,128]{1,0:T(8,128)S(1)} %cholesky.346), custom_call_target="Cholesky" | custom-call | tf_op jit(solution)/shard_map/jit(cholesky)/cholesky | solution.py:117
  319.8 10.0 %custom-call.15 = f32[1,128,128]{1,2,0:T(8,128)S(1)} custom-call(f32[1,128,128]{2,1,0:T(8,128)S(1)} %get-tuple-element.56), custom_call_target="InvertDiagBlocksLowerTriangular" | custom-call | tf_op jit(solution)/shard_map/jit(cholesky)/cholesky | solution.py:117
  330.8 1.1 convolution_subtract_fusion.1
  332.0 11.7 %cholesky.231 = f32[128,128]{1,0:T(8,128)S(1)} custom-call(f32[128,128]{1,0:T(8,128)S(1)} %convolution_subtract_fusion.1), custom_call_target="Cholesky" | custom-call | tf_op jit(solution)/shard_map/jit(cholesky)/cholesky | solution.py:117
  350.0 11.7 %cholesky.248 = f32[128,128]{1,0:T(8,128)S(1)} custom-call(f32[128,128]{1,0:T(8,128)S(1)} %cholesky.349), custom_call_target="Cholesky" | custom-call | tf_op jit(solution)/shard_map/jit(cholesky)/cholesky | solution.py:125
  361.7 9.8 %custom-call.16 = f32[1,128,128]{1,2,0:T(8,128)S(1)} custom-call(f32[1,128,128]{2,1,0:T(8,128)S(1)} %get-tuple-element.52), custom_call_target="InvertDiagBlocksLowerTriangular" | custom-call | tf_op jit(solution)/shard_map/jit(cholesky)/cholesky | solution.py:125
  372.6 1.1 slice_subtract_fusion.2
  373.7 11.9 %cholesky.265 = f32[128,128]{1,0:T(8,128)S(1)} custom-call(f32[128,128]{1,0:T(8,128)S(1)} %slice_subtract_fusion.2), custom_call_target="Cholesky" | custom-call | tf_op jit(solution)/shard_map/jit(cholesky)/cholesky | solution.py:125
  389.3 4.8 collective-permute-done.1
  396.8 11.7 %cholesky.282 = f32[128,128]{1,0:T(8,128)S(1)} custom-call(f32[128,128]{1,0:T(8,128)S(1)} %cholesky.352), custom_call_target="Cholesky" | custom-call | tf_op jit(solution)/shard_map/jit(cholesky)/cholesky | solution.py:125
  408.6 9.8 %custom-call.17 = f32[1,128,128]{1,2,0:T(8,128)S(1)} custom-call(f32[1,128,128]{2,1,0:T(8,128)S(1)} %get-tuple-element.48), custom_call_target="InvertDiagBlocksLowerTriangular" | custom-call | tf_op jit(solution)/shard_map/jit(cholesky)/cholesky | solution.py:125
  420.6 12.1 %cholesky.299 = f32[128,128]{1,0:T(8,128)S(1)} custom-call(f32[128,128]{1,0:T(8,128)S(1)} %slice_subtract_fusion.1), custom_call_target="Cholesky" | custom-call | tf_op jit(solution)/shard_map/jit(cholesky)/cholesky | solution.py:125
  435.3 1.4 collective-permute-start.2
  437.2 6.5 %collective-permute-done.2 = bf16[256,256]{1,0:T(8,128)(2,1)S(1)} collective-permute-done((bf16[256,256]{1,0:T(8,128)(2,1)S(1)}, bf16[256,256]{1,0:T(8,128)(2,1)S(1)}, u32[]{:S(2)}, u32[]{:S(2)}) %collective-permute-start.2) | collective-permute-done | bytes 131104 | tf_op jit(solution)/shard_map/ppermute | solution.py:9
  446.4 11.7 %cholesky.316 = f32[128,128]{1,0:T(8,128)S(1)} custom-call(f32[128,128]{1,0:T(8,128)S(1)} %cholesky.355), custom_call_target="Cholesky" | custom-call | tf_op jit(solution)/shard_map/jit(cholesky)/cholesky | solution.py:125
  458.2 9.8 %custom-call.18 = f32[1,128,128]{1,2,0:T(8,128)S(1)} custom-call(f32[1,128,128]{2,1,0:T(8,128)S(1)} %get-tuple-element.44), custom_call_target="InvertDiagBlocksLowerTriangular" | custom-call | tf_op jit(solution)/shard_map/jit(cholesky)/cholesky | solution.py:125
  470.2 11.9 %cholesky.333 = f32[128,128]{1,0:T(8,128)S(1)} custom-call(f32[128,128]{1,0:T(8,128)S(1)} %slice_subtract_fusion), custom_call_target="Cholesky" | custom-call | tf_op jit(solution)/shard_map/jit(cholesky)/cholesky | solution.py:125
  485.4 6.8 %while.1 = (s32[]{:T(128)}, f32[256,256]{1,0:T(8,128)}, s32[2,2]{1,0:T(2,128)S(1)}, f32[2,128,128]{2,1,0:T(8,128)}, s32[]{:T(128)}) while((s32[]{:T(128)}, f32[256,256]{1,0:T(8,128)}, s32[2,2]{1,0:T(2,128)S(1)}, f32[2,128,128]{2,1,0:T(8,128)}, s32[]{:T(128)}) %tuple.44), condition=%wide.while_cond, body=%wide.while_body.sunk | while | flops 2 | bytes 132205 | solution.py:126
  486.0 2.8 bitcast_dynamic-update-slice_fusion.2
  489.5 2.8 bitcast_dynamic-update-slice_fusion.2
  492.2 20.5 %custom-call.11 = f32[2,128,128]{1,2,0:T(8,128)S(1)} custom-call(f32[2,128,128]{2,1,0:T(8,128)} %get-tuple-element.13), custom_call_target="InvertDiagBlocksLowerTriangular" | custom-call | tf_op jit(solution)/shard_map/triangular_solve | solution.py:126
  512.7 1.6 fusion.12
  514.3 3.5 convolution_subtract_fusion
  517.8 1.6 fusion.66
  519.7 2.4 copy.69
  522.1 3.4 convolution_multiply_fusion.4
  525.5 1.6 fusion.20
  (106 shorter events, 29.4 us)
Async XLA Ops:
  7.2 4.5 copy-start
  7.2 85.9 %all-gather.3.cloned.1.call-start = ((), (), s32[]{:S(2)}) async-start(), calls=%async_computation.2 | async-start | bytes 4718592 | tf_op jit(solution)/shard_map/all_gather | solution.py:47
  9.4 102.9 %all-gather.5.cloned.1.call-start = ((), (), s32[]{:S(2)}) async-start(), calls=%async_computation.3 | async-start | bytes 4718592 | tf_op jit(solution)/shard_map/all_gather | solution.py:51
  11.6 2.1 copy-start.10
  11.6 286.1 %all-reduce.5.cloned.1.call-start = ((), (), s32[]{:S(2)}) async-start(), calls=%async_computation.6 | async-start | bytes 4194304 | tf_op jit(solution)/shard_map/psum | solution.py:93
  53.9 39.2 %copy-start.4 = (bf16[256,256]{1,0:T(8,128)(2,1)}, bf16[256,256]{1,0:T(8,128)(2,1)S(1)}, u32[]{:S(2)}) copy-start(bf16[256,256]{1,0:T(8,128)(2,1)S(1)} %all-reduce.6) | copy-start | bytes 393220
  112.3 4.9 copy-start.1
  119.2 406.3 %reduce-scatter.3.cloned.1.call-start = ((), (), s32[]{:S(2)}) async-start(), calls=%async_computation.4 | async-start | bytes 9437184 | tf_op jit(solution)/shard_map/reduce_scatter | solution.py:68
  176.1 5.3 copy-start.12
  176.1 5.3 copy-start.13
  176.1 351.9 %reduce-scatter.5.cloned.1.call-start = ((), (), s32[]{:S(2)}) async-start(), calls=%async_computation.5 | async-start | bytes 2621440 | tf_op jit(solution)/shard_map/reduce_scatter | solution.py:105
  178.8 6.2 %copy-start.11 = (s32[2,32]{1,0:T(2,128)S(1)}, s32[2,32]{1,0:T(2,128)}, u32[]{:S(2)}) copy-start(s32[2,32]{1,0:T(2,128)} %param.11) | copy-start | bytes 772
  289.3 4.5 copy-start.3
  307.3 0.7 copy-start.7
  345.7 1.5 collective-permute-start
  349.2 0.7 copy-start.8
  388.2 5.8 %collective-permute-start.1 = (bf16[256,256]{1,0:T(8,128)(2,1)S(1)}, bf16[256,256]{1,0:T(8,128)(2,1)S(1)}, u32[]{:S(2)}, u32[]{:S(2)}) collective-permute-start(bf16[256,256]{1,0:T(8,128)(2,1)S(1)} %fusion.46), channel_id=1, source_target_pairs={{0,2},{1,3},{2,0},{3,1},{4,6},{5,7},{6,4},{7,5},{8,10},{9,11},{10,... | collective-permute-start | bytes 393224 | tf_op jit(solution)/shard_map/ppermute | solution.py:9
  396.1 0.7 copy-start.9
  435.3 8.3 %collective-permute-start.2 = (bf16[256,256]{1,0:T(8,128)(2,1)S(1)}, bf16[256,256]{1,0:T(8,128)(2,1)S(1)}, u32[]{:S(2)}, u32[]{:S(2)}) collective-permute-start(bf16[256,256]{1,0:T(8,128)(2,1)S(1)} %fusion.43), channel_id=1, source_target_pairs={{0,4},{1,5},{2,6},{3,7},{4,0},{5,1},{6,2},{7,3},{8,12},{9,13},{10,... | collective-permute-start | bytes 393224 | tf_op jit(solution)/shard_map/ppermute | solution.py:9
  445.7 0.7 copy-start.6
  519.7 5.8 %copy-start.5 = (bf16[256,256]{1,0:T(8,128)(2,1)S(1)}, bf16[256,256]{1,0:T(8,128)(2,1)}, u32[]{:S(2)}) copy-start(bf16[256,256]{1,0:T(8,128)(2,1)} %copy-done.4) | copy-start | bytes 393220
  522.1 3.4 copy-start.2
Sparse Core Ops, SparseCore 0:
  10.2 53.7 all-gather.2
  66.2 46.1 all-gather.4
  119.3 68.2 all-reduce.4
  189.8 89.5 reduce-scatter.2
  297.8 34.5 reduce-scatter.4
where the time goes:
time: 541 us; the launch traced here: 535 us
  matrix products  231 us (43%)
  other arithmetic  169 us (31%)
  local copies, waits for them, and re-layouts  41.4 us (8%)
  blocking collectives  39.6 us (7%)
  waiting for transfers between devices  31.2 us (6%)
  between operations  19.6 us (4%)
    another operation x21, other arithmetic, shards(): lower_factor = jnp.linalg.cholesky(own_gram + partner_gram)  104 us
    dot_general x1, matrix products, shards(): lax.dot_general(gathered, effective, (((1,), (1,)), ((), ())), preferred_...  91.2 us
    dot_general x1, matrix products, shards(): lax.dot_general(effective, output_cotangent, (((0,), (1,)), ((), ())), pr...  56.7 us
    psum x1, blocking collectives, shards(): v_summed = lax.psum(v_partial, 'mp')  39.6 us
    dot_general x1, matrix products, shards(): lax.dot_general(placer, block_values.reshape(nb_local, block_size * block...  37 us
    another operation x6, other arithmetic, shards(): lower_factor = jnp.linalg.cholesky(gram_local)  34.1 us
    another operation x3, other arithmetic, shards(): lax.linalg.triangular_solve(lower_factor, moved_hidden, left_side=False,...  21.2 us
    all_gather x1, waiting for transfers between devices, shards(): model_rows = lax.all_gather(model_half, 'mp', axis=0, tiled=True)  19.2 us
  transfers between devices with their start and end apart: 8, of which 4 were waited for; matrix products, arithmetic and copies ran while one was open for 80% of the time, Pallas kernels for 0%

commit v1 on v0

--- a/solution.py
+++ b/solution.py
@@ -50,7 +50,7 @@
     v_partial = jnp.dot(output_cotangent, hidden_half, preferred_element_type=jnp.float32)
     model_rows = lax.all_gather(model_half, "mp", axis=0, tiled=True)
     u_summed = jnp.dot(gathered, model_rows, preferred_element_type=jnp.float32)
-    v_summed = lax.psum(v_partial, "mp")
+    v_summed = jnp.sum(lax.all_gather(v_partial, "mp"), axis=0)
     left_factor_shard = u_summed.astype(jnp.bfloat16)
     right_factor_shard = v_summed.astype(jnp.bfloat16)
     base_projection_output = lax.dot_general(

time: 541 us -> 663 us (1.23)
  matrix products: 231 us -> 301 us
  waiting for transfers between devices: 31.2 us -> 100 us
  blocking collectives: 39.6 us -> 0 us
  other arithmetic: 169 us -> 194 us
    dot_general x1, matrix products: 56.7 us -> 124 us  [shards(): lax.dot_general(effective, output_cotangent, (((0,), (1,)), ((), ())), pr...]
    all_gather x1, waiting for transfers between devices: 0.01 us -> 40.1 us  [shards(): gathered = lax.all_gather(tokens, 'mp', axis=1, tiled=True)]
    psum x1 -> x0, blocking collectives: 39.6 us -> none  [shards(): v_summed = lax.psum(v_partial, 'mp')]
    all_gather x1, waiting for transfers between devices: 19.2 us -> 47.9 us  [shards(): model_rows = lax.all_gather(model_half, 'mp', axis=0, tiled=True)]
    another operation x21, other arithmetic: 104 us -> 122 us  [shards(): lower_factor = jnp.linalg.cholesky(own_gram + partner_gram)]
    unnamed x33 -> x31, local copies, waits for them, and re-layouts: 13.6 us -> 10.5 us
  transfers between devices with their start and end apart: 8 -> 9, of which waited for: 4 -> 5; matrix products, arithmetic and copies ran while one was open for 80% -> 79% of each run, Pallas kernels for 0% -> 0%
where the time goes in v1:
time: 663 us; the launch traced here: 656 us
  matrix products  301 us (45%)
  other arithmetic  194 us (29%)
  waiting for transfers between devices  100 us (15%)
  local copies, waits for them, and re-layouts  38.1 us (6%)
  between operations  20.2 us (3%)
    dot_general x1, matrix products, shards(): lax.dot_general(effective, output_cotangent, (((0,), (1,)), ((), ())), pr...  124 us
    another operation x21, other arithmetic, shards(): lower_factor = jnp.linalg.cholesky(own_gram + partner_gram)  122 us
    dot_general x1, matrix products, shards(): lax.dot_general(gathered, effective, (((1,), (1,)), ((), ())), preferred_...  92.1 us
    all_gather x1, waiting for transfers between devices, shards(): model_rows = lax.all_gather(model_half, 'mp', axis=0, tiled=True)  47.9 us
    another operation x6, other arithmetic, shards(): lower_factor = jnp.linalg.cholesky(gram_local)  40.2 us
    all_gather x1, waiting for transfers between devices, shards(): gathered = lax.all_gather(tokens, 'mp', axis=1, tiled=True)  40.1 us
    dot_general x1, matrix products, shards(): lax.dot_general(placer, block_values.reshape(nb_local, block_size * block...  35.4 us
    another operation x3, other arithmetic, shards(): lax.linalg.triangular_solve(lower_factor, moved_hidden, left_side=False,...  21.8 us
  transfers between devices with their start and end apart: 9, of which 5 were waited for; matrix products, arithmetic and copies ran while one was open for 79% of the time, Pallas kernels for 0%

profile of v1, /device:TPU:0, one launch (start us, length us, event | category | flops | bytes accessed | tf_op | source)
XLA Modules:
  0.0 655.8 jit_solution(8657644360949495767)
XLA Ops:
  7.2 3.7 fusion.29
  13.1 35.4 %fusion.23 = f32[24,64,128,128]{3,1,2,0:T(8,128)} fusion(s32[24,64]{1,0:T(8,128)S(1)} %multiply_add_fusion, s32[32]{0:T(128)S(1)} %get-tuple-element.61, bf16[4,8,128,128]{3,2,1,0:T(8,128)(2,1)S(1)} %bitcast.156), kind=kOutput, calls=%fused_computation.40 | convolution fusion | flops 1610661888 | bytes 101718144 | tf_op jit(solution)/shard_map/dot_general | solution.py:35
  48.5 1.7 reduce_sum.9
  51.4 40.1 %all-gather.5.cloned.1.call-done = bf16[256,8192]{0,1:T(8,128)(2,1)} async-done(((bf16[256,1024]{0,1:T(8,128)(2,1)}), bf16[256,8192]{0,1:T(8,128)(2,1)}) %all-gather.5.cloned.1.call-update) | async-done | bytes 4194320 | tf_op jit(solution)/shard_map/all_gather | solution.py:47
  91.5 47.9 %all-gather.7.cloned.1.call-done = bf16[8192,256]{1,0:T(8,128)(2,1)} async-done(((bf16[1024,256]{1,0:T(8,128)(2,1)}), bf16[8192,256]{1,0:T(8,128)(2,1)}) %all-gather.7.cloned.1.call-update) | async-done | bytes 4194320 | tf_op jit(solution)/shard_map/all_gather | solution.py:51
  139.4 4.8 convolution_convert_fusion
  144.2 1.9 fusion.4
  146.2 124.0 %fusion.106 = f32[8192,256]{1,0:T(8,128)} fusion(bf16[256,3072]{1,0:T(8,128)(2,1)S(1)} %copy-done.1, f32[384,8,64,128]{3,2,1,0:T(8,128)} %bitcast.43, bf16[3072,8192]{1,0:T(8,128)(2,1)} %param.9), kind=kOutput, calls=%fused_computation.165 | convolution fusion | flops 12960399360 | bytes 160956416 | tf_op jit(solution)/shard_map/dot_general | solution.py:69
  271.9 2.2 gather_fusion
  274.1 92.1 %convolution_bitcast_fusion = f32[256,3072]{0,1:T(8,128)} fusion(bf16[256,8192]{0,1:T(8,128)(2,1)} %all-gather.5.cloned.1.call-done, f32[384,8,64,128]{3,2,1,0:T(8,128)} %bitcast.43, bf16[3072,8192]{1,0:T(8,128)(2,1)} %param.9), kind=kOutput, calls=%fused_computation.6 | convolution fusion | flops 12960399360 | bytes 158334976 | tf_op jit(solution)/shard_map/dot_general | solution.py:56
  366.2 3.7 fusion.2
  369.9 2.6 copy.67
  372.5 6.4 copy.53
  378.8 4.5 gather_fusion.1
  383.3 3.9 fusion.14
  387.3 2.7 multiply_subtract_fusion
  389.9 5.1 fusion.110
  397.6 12.3 %cholesky.214 = f32[128,128]{1,0:T(8,128)} custom-call(f32[128,128]{1,0:T(8,128)S(1)} %cholesky.346), custom_call_target="Cholesky" | custom-call | tf_op jit(solution)/shard_map/jit(cholesky)/cholesky | solution.py:117
  412.3 11.7 %custom-call.15 = f32[1,128,128]{1,2,0:T(8,128)} custom-call(f32[1,128,128]{2,1,0:T(8,128)} %get-tuple-element.56), custom_call_target="InvertDiagBlocksLowerTriangular" | custom-call | tf_op jit(solution)/shard_map/jit(cholesky)/cholesky | solution.py:117
  425.1 1.7 convolution_subtract_fusion.1
  426.8 13.2 %cholesky.231 = f32[128,128]{1,0:T(8,128)} custom-call(f32[128,128]{1,0:T(8,128)} %convolution_subtract_fusion.1), custom_call_target="Cholesky" | custom-call | tf_op jit(solution)/shard_map/jit(cholesky)/cholesky | solution.py:117
  447.0 12.3 %cholesky.248 = f32[128,128]{1,0:T(8,128)} custom-call(f32[128,128]{1,0:T(8,128)S(1)} %cholesky.349), custom_call_target="Cholesky" | custom-call | tf_op jit(solution)/shard_map/jit(cholesky)/cholesky | solution.py:125
  460.2 1.5 fusion.88
  461.7 11.3 %custom-call.16 = f32[1,128,128]{1,2,0:T(8,128)} custom-call(f32[1,128,128]{2,1,0:T(8,128)} %get-tuple-element.52), custom_call_target="InvertDiagBlocksLowerTriangular" | custom-call | tf_op jit(solution)/shard_map/jit(cholesky)/cholesky | solution.py:125
  474.1 1.7 slice_subtract_fusion.2
  475.8 13.3 %cholesky.265 = f32[128,128]{1,0:T(8,128)} custom-call(f32[128,128]{1,0:T(8,128)} %slice_subtract_fusion.2), custom_call_target="Cholesky" | custom-call | tf_op jit(solution)/shard_map/jit(cholesky)/cholesky | solution.py:125
  493.4 5.0 collective-permute-done.1
  501.2 12.3 %cholesky.282 = f32[128,128]{1,0:T(8,128)} custom-call(f32[128,128]{1,0:T(8,128)S(1)} %cholesky.352), custom_call_target="Cholesky" | custom-call | tf_op jit(solution)/shard_map/jit(cholesky)/cholesky | solution.py:125
  514.4 1.5 fusion.86
  515.9 11.3 %custom-call.17 = f32[1,128,128]{1,2,0:T(8,128)} custom-call(f32[1,128,128]{2,1,0:T(8,128)} %get-tuple-element.48), custom_call_target="InvertDiagBlocksLowerTriangular" | custom-call | tf_op jit(solution)/shard_map/jit(cholesky)/cholesky | solution.py:125
  528.2 1.7 slice_subtract_fusion.1
  530.0 13.4 %cholesky.299 = f32[128,128]{1,0:T(8,128)} custom-call(f32[128,128]{1,0:T(8,128)} %slice_subtract_fusion.1), custom_call_target="Cholesky" | custom-call | tf_op jit(solution)/shard_map/jit(cholesky)/cholesky | solution.py:125
  548.6 6.6 %collective-permute-done.2 = bf16[256,256]{1,0:T(8,128)(2,1)S(1)} collective-permute-done((bf16[256,256]{1,0:T(8,128)(2,1)S(1)}, bf16[256,256]{1,0:T(8,128)(2,1)S(1)}, u32[]{:S(2)}, u32[]{:S(2)}) %collective-permute-start.2) | collective-permute-done | bytes 131104 | tf_op jit(solution)/shard_map/ppermute | solution.py:9
  557.9 12.3 %cholesky.316 = f32[128,128]{1,0:T(8,128)} custom-call(f32[128,128]{1,0:T(8,128)S(1)} %cholesky.355), custom_call_target="Cholesky" | custom-call | tf_op jit(solution)/shard_map/jit(cholesky)/cholesky | solution.py:125
  571.1 1.5 select_reduce_fusion.1
  572.6 11.3 %custom-call.18 = f32[1,128,128]{1,2,0:T(8,128)} custom-call(f32[1,128,128]{2,1,0:T(8,128)} %get-tuple-element.44), custom_call_target="InvertDiagBlocksLowerTriangular" | custom-call | tf_op jit(solution)/shard_map/jit(cholesky)/cholesky | solution.py:125
  585.0 1.7 slice_subtract_fusion
  586.7 13.4 %cholesky.333 = f32[128,128]{1,0:T(8,128)} custom-call(f32[128,128]{1,0:T(8,128)} %slice_subtract_fusion), custom_call_target="Cholesky" | custom-call | tf_op jit(solution)/shard_map/jit(cholesky)/cholesky | solution.py:125
  604.4 6.8 %while.1 = (s32[]{:T(128)}, f32[256,256]{1,0:T(8,128)}, s32[2,2]{1,0:T(2,128)S(1)}, f32[2,128,128]{2,1,0:T(8,128)}, s32[]{:T(128)}) while((s32[]{:T(128)}, f32[256,256]{1,0:T(8,128)}, s32[2,2]{1,0:T(2,128)S(1)}, f32[2,128,128]{2,1,0:T(8,128)}, s32[]{:T(128)}) %tuple.44), condition=%wide.while_cond, body=%wide.while_body.sunk | while | flops 2 | bytes 132205 | solution.py:126
  605.0 2.8 bitcast_dynamic-update-slice_fusion.2
  608.4 2.8 bitcast_dynamic-update-slice_fusion.2
  611.2 21.1 %custom-call.11 = f32[2,128,128]{1,2,0:T(8,128)} custom-call(f32[2,128,128]{2,1,0:T(8,128)} %get-tuple-element.13), custom_call_target="InvertDiagBlocksLowerTriangular" | custom-call | tf_op jit(solution)/shard_map/triangular_solve | solution.py:126
  632.3 2.4 fusion.12
  634.7 3.5 convolution_subtract_fusion
  638.3 1.6 fusion.66
  640.2 2.4 copy.69
  642.5 3.4 convolution_multiply_fusion.4
  646.0 1.6 fusion.20
  (107 shorter events, 40.2 us)
Async XLA Ops:
  7.2 3.9 copy-start.5
  7.2 5.0 copy-start.3
  7.2 41.3 %all-gather.9.cloned.1.call-start = ((), (), s32[]{:S(2)}) async-start(), calls=%async_computation.6 | async-start | bytes 2359296 | tf_op jit(solution)/shard_map/all_gather | solution.py:53
  11.0 2.1 copy-start.12
  11.0 2.1 copy-start.6
  11.0 80.5 %all-gather.5.cloned.1.call-start = ((), (), s32[]{:S(2)}) async-start(), calls=%async_computation.2 | async-start | bytes 4718592 | tf_op jit(solution)/shard_map/all_gather | solution.py:47
  12.1 127.3 %all-gather.7.cloned.1.call-start = ((), (), s32[]{:S(2)}) async-start(), calls=%async_computation.3 | async-start | bytes 4718592 | tf_op jit(solution)/shard_map/all_gather | solution.py:51
  13.0 374.2 %all-reduce.4.cloned.1.call-start = ((), (), s32[]{:S(2)}) async-start(), calls=%async_computation.7 | async-start | bytes 4194304 | tf_op jit(solution)/shard_map/psum | solution.py:93
  51.4 92.8 %copy-start.1 = (bf16[256,3072]{1,0:T(8,128)(2,1)S(1)}, bf16[256,3072]{1,0:T(8,128)(2,1)}, u32[]{:S(2)}) copy-start(bf16[256,3072]{1,0:T(8,128)(2,1)} %param.14) | copy-start | bytes 4718596
  146.1 499.8 %reduce-scatter.3.cloned.1.call-start = ((), (), s32[]{:S(2)}) async-start(), calls=%async_computation.4 | async-start | bytes 9437184 | tf_op jit(solution)/shard_map/reduce_scatter | solution.py:68
  270.2 378.3 %reduce-scatter.5.cloned.1.call-start = ((), (), s32[]{:S(2)}) async-start(), calls=%async_computation.5 | async-start | bytes 2621440 | tf_op jit(solution)/shard_map/reduce_scatter | solution.py:105
  274.1 92.1 %copy-start = (f32[3072,256]{1,0:T(8,128)S(1)}, f32[3072,256]{1,0:T(8,128)}, u32[]{:S(2)}) copy-start(f32[3072,256]{1,0:T(8,128)} %param.13) | copy-start | bytes 9437188
  378.8 4.5 copy-start.4
  396.9 0.7 copy-start.8
  442.9 1.4 collective-permute-start
  446.3 0.7 copy-start.9
  492.6 5.8 collective-permute-start.1
  500.5 0.7 copy-start.10
  546.8 8.3 %collective-permute-start.2 = (bf16[256,256]{1,0:T(8,128)(2,1)S(1)}, bf16[256,256]{1,0:T(8,128)(2,1)S(1)}, u32[]{:S(2)}, u32[]{:S(2)}) collective-permute-start(bf16[256,256]{1,0:T(8,128)(2,1)S(1)} %fusion.43), channel_id=1, source_target_pairs={{0,4},{1,5},{2,6},{3,7},{4,0},{5,1},{6,2},{7,3},{8,12},{9,13},{10,... | collective-permute-start | bytes 393224 | tf_op jit(solution)/shard_map/ppermute | solution.py:9
  557.2 0.7 copy-start.7
  634.7 3.6 copy-start.11
  642.5 3.4 copy-start.2
Sparse Core Ops, SparseCore 0:
  11.1 31.8 all-gather.8
  45.2 46.2 all-gather.4
  93.7 45.6 all-gather.6
  146.2 68.2 all-reduce.3
  270.3 88.2 reduce-scatter.2
  387.4 34.0 reduce-scatter.4
